TPU v7x, 256 devices: a whole 4x4x8 slice. The times are simulated.
256 devices in a mesh: space: 128 (over x, y, z), rep: 2 (over core).
Axes of the slice: x: 4, y: 4, z: 8, core: 2. Of those that a mesh axis runs over, the one named last changes fastest.
Arguments:
- acts: bfloat16 [3072, 512, 128], P(('space', 'rep')), may hold values from -6 to 6
- preact: bfloat16 [3072, 512, 128], P(('space', 'rep')), may hold values from -8 to 8
- cotangent: bfloat16 [3072, 512, 128], P(('space', 'rep')), may hold values from -6 to 6
- filt: bfloat16 [3456, 128], P('space', 'rep'), may hold values from -0.109375 to 0.109375
- counts: int32 [256], replicated, may hold values from 1 to 12, as said below
- neighbors: int32 [3072, 27], P(('space', 'rep')), may hold values from 0 to 3072, as said below
Outputs:
- input_grad: bfloat16 [3072, 512, 128], P(('space', 'rep'))
- filt_grad: float32 [3456, 128], P('space', 'rep')
Inputs may be any that keep to these rules, and one draw needn't show every extreme that they name: counts[d] is the number of live bricks of device d, which fill its first slots; counts[d] + counts[d xor 1] <= 16, where d xor 1 is the other core of the same chip; in every draw some device holds 12 bricks and its partner 2 * 8 - 12. Brick n = d * 12 + s sits in slab d of the brick grid at one of 5 x 5 places, slot 0 of every device at the middle place; neighbors[n, k] is the index of the live brick at offset off_k (first component along the slabs, so it lies on device d - 1, d or d + 1) from that place, or 3072 where there is none, also for bricks that are not live.
All inputs are finite; a program needn't handle non-finite values.
Results may differ from a plain program's by a relative error of at most 0.0049.
Values may be sent and summed in bfloat16 or wider, within the bound.
A program may use at most 128 MiB of HBM per device.

v0:
```python
import math
import jax
import jax.numpy as jnp
from jax import lax
from jax.sharding import PartitionSpec as P

BRICK = 8
tap_offsets = [
    (step_x, step_y, step_z)
    for step_x in (-1, 0, 1)
    for step_y in (-1, 0, 1)
    for step_z in (-1, 0, 1)
]


def shifted(x, axis, by):
    count = lax.axis_size(axis)
    pairs = [(i, i + by) for i in range(count) if 0 <= i + by < count]
    return lax.ppermute(x, axis, pairs)


def silu_slope(values):
    sigma = jax.nn.sigmoid(values)
    return sigma * (1.0 + values * (1.0 - sigma))


def edge(offset, brick_side):
    if offset < 0:
        return slice(brick_side - 1, brick_side)
    if offset == 0:
        return slice(0, brick_side)
    return slice(0, 1)


def assemble(planes, indices, usable):
    layers = []
    for step_x in range(3):
        strips = []
        for step_y in range(3):
            columns = []
            for step_z in range(3):
                tap = step_x * 9 + step_y * 3 + step_z
                source = planes[step_x]
                brick_side = source.shape[2]
                fetched = jnp.take(source, indices[:, tap], axis=0)
                fetched = fetched[:, :, edge(step_y - 1, brick_side), edge(step_z - 1, brick_side)]
                keeper = usable[:, tap][:, None, None, None, None]
                columns.append(jnp.where(keeper, fetched, jnp.zeros_like(fetched)))
            strips.append(jnp.concatenate(columns, axis=3))
        layers.append(jnp.concatenate(strips, axis=2))
    return jnp.concatenate(layers, axis=1)


def unfold(padded, direction):
    brick_side = padded.shape[0] - 2
    sections = []
    for step_x, step_y, step_z in tap_offsets:
        start_x = 1 + direction * step_x
        start_y = 1 + direction * step_y
        start_z = 1 + direction * step_z
        sections.append(
            padded[
                start_x : start_x + brick_side,
                start_y : start_y + brick_side,
                start_z : start_z + brick_side,
            ]
        )
    return jnp.concatenate(sections, axis=-1).reshape(brick_side**3, -1)


def run_bricks(act_pad, grad_pad, filt_flip, running):

    def per_brick(accum, operands):
        act_block, grad_block = operands
        unrolled_act = unfold(act_block, 1)
        unrolled_grad = unfold(grad_block, -1)
        center = grad_block[1:-1, 1:-1, 1:-1].reshape(-1, grad_block.shape[-1])
        accum = accum + lax.dot_general(
            unrolled_act, center, (((0,), (0,)), ((), ())), preferred_element_type=jnp.float32
        )
        return (accum, jnp.dot(unrolled_grad, filt_flip, preferred_element_type=jnp.float32))

    return lax.scan(per_brick, running, (act_pad, grad_pad))


def on_device(acts, preact, cotangent, filt, counts, neighbors):
    slot_count, voxels, channels = acts.shape
    devices = lax.axis_size(("space", "rep"))
    position = lax.axis_index(("space", "rep"))
    grand_total = slot_count * devices
    live_count = counts[position]
    is_live = jnp.arange(slot_count) < live_count
    grad_pre = jnp.where(
        is_live[:, None, None],
        cotangent.astype(jnp.float32) * silu_slope(preact.astype(jnp.float32)),
        0.0,
    ).astype(jnp.bfloat16)
    gathered_rows = lax.all_gather(filt, "space", axis=0, tiled=True)
    full_filter = lax.all_gather(gathered_rows, "rep", axis=1, tiled=True)
    filt_flip = (
        full_filter.reshape(27, channels, channels)
        .transpose(0, 2, 1)
        .reshape(27 * channels, channels)
    )
    act_five = acts.reshape(slot_count, BRICK, BRICK, BRICK, channels)
    grad_five = grad_pre.reshape(slot_count, BRICK, BRICK, BRICK, channels)
    from_below = shifted((act_five[:, BRICK - 1 :], grad_five[:, BRICK - 1 :]), ("space", "rep"), 1)
    from_above = shifted((act_five[:, :1], grad_five[:, :1]), ("space", "rep"), -1)
    usable = neighbors < grand_total
    slab_step = jnp.arange(27, dtype=jnp.int32) // 9 - 1
    local_slot = jnp.clip(
        neighbors - (position + slab_step[None, :]) * slot_count, 0, slot_count - 1
    )
    act_pad = assemble((from_below[0], act_five, from_above[0]), local_slot, usable)
    grad_pad = assemble((from_below[1], grad_five, from_above[1]), local_slot, usable)
    start = jnp.zeros((27 * channels, channels), jnp.float32)
    filt_sum, grads = run_bricks(act_pad, grad_pad, filt_flip, start)
    brick_grads = grads.astype(jnp.bfloat16)
    input_grad = jnp.where(is_live[:, None, None], brick_grads, jnp.zeros_like(brick_grads))
    inverse_norm = 1.0 / math.sqrt(grand_total * voxels)
    shard_rows = lax.psum_scatter(filt_sum, "space", scatter_dimension=0, tiled=True)
    filt_grad = lax.psum_scatter(shard_rows, "rep", scatter_dimension=1, tiled=True)
    return (input_grad, filt_grad * inverse_norm)


def solution(mesh):
    in_specs = (
        P(("space", "rep"), None, None),
        P(("space", "rep"), None, None),
        P(("space", "rep"), None, None),
        P("space", "rep"),
        P(),
        P(("space", "rep"), None),
    )
    out_specs = (P(("space", "rep"), None, None), P("space", "rep"))
    return jax.shard_map(
        on_device, mesh=mesh, in_specs=in_specs, out_specs=out_specs, check_vma=False
    )
```

profile of v0, /device:TPU:1, one launch (start us, length us, event | category | flops | bytes accessed | tf_op | source)
XLA Modules:
  0.0 1390.8 jit_solution(1618855230662512076)
XLA Ops:
  9.3 3.3 fusion.11
  13.4 5.1 collective-permute-start.3
  21.2 3.6 collective-permute-start.2
  38.6 2.0 gather_fusion.12
  41.3 2.0 gather_fusion.41
  52.7 2.0 gather_fusion.43
  54.7 2.0 gather_fusion.16
  65.9 2.0 gather_fusion.11
  70.8 2.0 gather_fusion.42
  94.1 2.0 gather_fusion.40
  112.0 295.4 %all-gather = bf16[128,27,64]{2,1,0:T(8,128)(2,1)S(1)} all-gather(bf16[1,27,64]{2,1,0:T(8,128)(2,1)S(1)} %bitcast.211), channel_id=1, replica_groups=mesh['space'=128,'rep'=2] {'space'}, dimensions={0}, use_global_device_ids=true | all-gather | bytes 445824 | tf_op jit(solution)/shard_map/all_gather | solution.py:98
  408.1 58.8 %all_gather.7 = bf16[3456,128]{0,1:T(8,128)(2,1)S(1)} all-gather(bf16[3456,64]{0,1:T(8,128)(2,1)S(1)} %copy.9), channel_id=1, replica_groups=mesh['space'=128,'rep'=2] {'rep'}, dimensions={1}, use_global_device_ids=true | all-gather | bytes 1327104 | tf_op jit(solution)/shard_map/all_gather | solution.py:99
  469.3 3.5 select_select_fusion
  472.9 4.8 broadcast_select_fusion.4
  477.7 2.3 fusion.12
  480.0 2.2 broadcast_select_fusion.32
  482.2 2.2 broadcast_select_fusion.28
  487.5 2.2 gather_fusion.21
  489.7 2.2 gather_fusion.23
  493.1 2.2 gather_fusion.19
  496.5 2.2 gather_fusion.25
  499.9 2.2 gather_fusion.18
  503.4 2.2 gather_fusion.20
  506.8 2.2 gather_fusion.24
  510.2 2.2 gather_fusion.26
  514.9 2.2 gather_fusion.5
  517.1 2.2 gather_fusion.3
  520.5 2.2 gather_fusion.7
  523.9 2.2 gather_fusion.1
  527.3 2.2 gather_fusion.6
  530.8 2.2 gather_fusion.8
  534.2 2.2 gather_fusion
  537.6 2.2 gather_fusion.22
  541.2 2.3 gather_fusion.4
  544.8 2.2 gather_fusion.2
  559.2 8.8 maximum_maximum_fusion.1
  568.0 6.8 maximum_maximum_fusion
  574.8 353.8 %while.14 = (s32[]{:T(128)}, f32[3456,128]{1,0:T(8,128)}, bf16[12,512,128]{2,1,0:T(8,128)(2,1)}, bf16[12,10,10,10,128]{4,3,2,1,0:T(8,128)(2,1)}, bf16[12,10,10,1...) while((s32[]{:T(128)}, f32[3456,128]{1,0:T(8,128)}, ...), condition=%wide.region_1.4_spmd.clone.clone, body=%wide.region_0.3_spmd.clone.sunk.clone | while | flops 906854400 | bytes 41230984 | solution.py:83
  598.9 4.2 fusion.52
  628.4 4.2 fusion.52
  657.9 4.2 fusion.52
  687.4 4.2 fusion.52
  716.8 4.2 fusion.52
  746.3 4.2 fusion.52
  775.8 4.2 fusion.52
  805.3 4.2 fusion.52
  834.8 4.2 fusion.52
  864.2 4.2 fusion.52
  893.7 4.2 fusion.52
  923.2 4.2 fusion.52
  928.6 296.9 %fusion = f32[32,128]{1,0:T(8,128)S(1)} fusion(f32[3456,128]{1,0:T(8,128)} %get-tuple-element.38), kind=kCustom, calls=%all-reduce-scatter | all-reduce-scatter fusion | flops 524289 | bytes 1786880
  1234.1 7.0 collective-permute-start.15
  1243.7 5.8 collective-permute-start.18
  1249.5 22.4 %collective-permute-start.19 = (f32[32,128]{1,0:T(8,128)S(1)}, f32[32,128]{1,0:T(8,128)S(1)}, u32[]{:S(2)}, u32[]{:S(2)}) collective-permute-start(f32[32,128]{1,0:T(8,128)S(1)} %fusion), channel_id=1, source_target_pairs={{0,32},{2,34},{4,36},{6,38},{8,40},{10,42},{12,44},{14,46},{16,48}... | collective-permute-start | bytes 49160
  1272.0 2.5 collective-permute-start.20
  1274.5 7.8 collective-permute-start.21
  1282.4 4.9 collective-permute-start.22
  1287.3 2.2 collective-permute-start.4
  1291.5 4.6 collective-permute-start.6
  1296.1 4.3 collective-permute-start.7
  1300.4 4.0 collective-permute-start.8
  1304.4 2.2 collective-permute-start.9
  1308.0 2.6 concatenate.112
  1312.7 69.8 %reduce-scatter.6.cloned.1.call-done = f32[64,27]{1,0:T(8,128)} async-done(((f32[128,27]{1,0:T(8,128)}), f32[64,27]{1,0:T(8,128)}) %reduce-scatter.6.cloned.1.call-update) | async-done | bytes 6928
  (990 shorter events, 435.4 us)
Async XLA Ops:
  7.2 11.3 copy-start
  7.2 19.6 %copy-start.14 = (s32[12,27]{1,0:T(8,128)S(1)}, s32[12,27]{1,0:T(8,128)}, u32[]{:S(2)}) copy-start(s32[12,27]{1,0:T(8,128)} %param.17) | copy-start | bytes 3892
  7.2 1375.3 %reduce-scatter.6.cloned.1.call-start = ((), (), s32[]{:S(2)}) async-start(), calls=%async_computation.1 | async-start | bytes 98304
  7.2 22.8 %copy-start.15 = (s32[12,27]{1,0:T(8,128)S(1)}, s32[12,27]{1,0:T(8,128)}, u32[]{:S(2)}) copy-start(s32[12,27]{1,0:T(8,128)} %param.17) | copy-start | bytes 3892
  13.4 471.6 %collective-permute-start.3 = (bf16[12,1,8,8,128]{4,3,2,1,0:T(8,128)(2,1)}, bf16[12,1,8,8,128]{4,3,2,1,0:T(8,128)(2,1)S(1)}, u32[]{:S(2)}, u32[]{:S(2)}) collective-permute-start(bf16[12,1,8,8,128]{4,3,2,1,0:T(8,128)(2,1)} %get-tuple-element.129), channel_id=1, source_target_pairs={{1,0},{2,1},{3,2},{4,3},{5,4},{6,5},{7,6},{8,7},{9,8},{10,9},{11,1... | collective-permute-start | bytes 589832 | tf_op jit(solution)/shard_map/ppermute | solution.py:19
  19.3 468.2 %collective-permute-start.1 = (bf16[12,1,8,8,128]{4,3,2,1,0:T(8,128)(2,1)}, bf16[12,1,8,8,128]{4,3,2,1,0:T(8,128)(2,1)}, u32[]{:S(2)}, u32[]{:S(2)}) collective-permute-start(bf16[12,1,8,8,128]{4,3,2,1,0:T(8,128)(2,1)} %get-tuple-element.131), channel_id=1, source_target_pairs={{1,0},{2,1},{3,2},{4,3},{5,4},{6,5},{7,6},{8,7},{9,8},{10,9},{11,1... | collective-permute-start | bytes 589832 | tf_op jit(solution)/shard_map/ppermute | solution.py:19
  21.2 491.2 %collective-permute-start.2 = (bf16[12,1,8,8,128]{4,3,2,1,0:T(8,128)(2,1)}, bf16[12,1,8,8,128]{4,3,2,1,0:T(8,128)(2,1)S(1)}, u32[]{:S(2)}, u32[]{:S(2)}) collective-permute-start(bf16[12,1,8,8,128]{4,3,2,1,0:T(8,128)(2,1)} %get-tuple-element.128), channel_id=1, source_target_pairs={{0,1},{1,2},{2,3},{3,4},{4,5},{5,6},{6,7},{7,8},{8,9},{9,10},{10,1... | collective-permute-start | bytes 589832 | tf_op jit(solution)/shard_map/ppermute | solution.py:19
  24.8 490.1 %collective-permute-start = (bf16[12,1,8,8,128]{4,3,2,1,0:T(8,128)(2,1)}, bf16[12,1,8,8,128]{4,3,2,1,0:T(8,128)(2,1)}, u32[]{:S(2)}, u32[]{:S(2)}) collective-permute-start(bf16[12,1,8,8,128]{4,3,2,1,0:T(8,128)(2,1)} %get-tuple-element.130), channel_id=1, source_target_pairs={{0,1},{1,2},{2,3},{3,4},{4,5},{5,6},{6,7},{7,8},{8,9},{9,10},{10,1... | collective-permute-start | bytes 589832 | tf_op jit(solution)/shard_map/ppermute | solution.py:19
  27.8 8.8 copy-start.43
  82.4 29.6 %copy-start.29 = (s32[12]{0:T(128)}, s32[12]{0:T(128)S(1)}, u32[]{:S(2)}) copy-start(s32[12]{0:T(128)S(1)} %get-tuple-element.86) | copy-start | bytes 148
  82.4 29.6 %copy-start.16 = (bf16[27,64]{1,0:T(8,128)(2,1)S(1)}, bf16[27,64]{1,0:T(8,128)(2,1)}, u32[]{:S(2)}) copy-start(bf16[27,64]{1,0:T(8,128)(2,1)} %param.15) | copy-start | bytes 10372
  407.7 61.5 %copy-start.35 = (pred[12]{0:T(512)(128)(4,1)S(1)}, pred[12]{0:T(512)(128)(4,1)}, u32[]{:S(2)}) copy-start(pred[12]{0:T(512)(128)(4,1)} %get-tuple-element.101) | copy-start | bytes 40
  407.7 61.5 %copy-start.36 = (pred[12]{0:T(512)(128)(4,1)S(1)}, pred[12]{0:T(512)(128)(4,1)}, u32[]{:S(2)}) copy-start(pred[12]{0:T(512)(128)(4,1)} %get-tuple-element.202) | copy-start | bytes 40
  472.8 9.4 copy-start.23
  472.8 9.4 copy-start.24
  472.8 9.4 copy-start.41
  472.8 9.4 copy-start.42
  472.8 11.6 copy-start.30
  522.7 28.5 %copy-start.21 = (pred[12]{0:T(512)(128)(4,1)S(1)}, pred[12]{0:T(512)(128)(4,1)}, u32[]{:S(2)}) copy-start(pred[12]{0:T(512)(128)(4,1)} %get-tuple-element.91) | copy-start | bytes 40
  522.7 28.5 %copy-start.22 = (pred[12]{0:T(512)(128)(4,1)S(1)}, pred[12]{0:T(512)(128)(4,1)}, u32[]{:S(2)}) copy-start(pred[12]{0:T(512)(128)(4,1)} %get-tuple-element.93) | copy-start | bytes 40
  523.9 28.8 %copy-start.19 = (pred[12]{0:T(512)(128)(4,1)S(1)}, pred[12]{0:T(512)(128)(4,1)}, u32[]{:S(2)}) copy-start(pred[12]{0:T(512)(128)(4,1)} %get-tuple-element.89) | copy-start | bytes 40
  523.9 28.9 %copy-start.20 = (pred[12]{0:T(512)(128)(4,1)S(1)}, pred[12]{0:T(512)(128)(4,1)}, u32[]{:S(2)}) copy-start(pred[12]{0:T(512)(128)(4,1)} %get-tuple-element.95) | copy-start | bytes 40
  526.1 28.6 %copy-start.17 = (pred[12]{0:T(512)(128)(4,1)S(1)}, pred[12]{0:T(512)(128)(4,1)}, u32[]{:S(2)}) copy-start(pred[12]{0:T(512)(128)(4,1)} %get-tuple-element.88) | copy-start | bytes 40
  526.1 28.6 %copy-start.18 = (pred[12]{0:T(512)(128)(4,1)S(1)}, pred[12]{0:T(512)(128)(4,1)}, u32[]{:S(2)}) copy-start(pred[12]{0:T(512)(128)(4,1)} %get-tuple-element.90) | copy-start | bytes 40
  537.6 21.4 %copy-start.5 = (bf16[12,8,8,1,128]{4,3,2,1,0:T(2,128)(2,1)S(1)}, bf16[12,8,8,1,128]{4,3,2,1,0:T(2,128)(2,1)}, u32[]{:S(2)}) copy-start(bf16[12,8,8,1,128]{4,3,2,1,0:T(2,128)(2,1)} %get-tuple-element.160) | copy-start | bytes 589828
  544.8 14.3 %copy-start.9 = (bf16[12,8,1,8,128]{4,3,2,1,0:T(8,128)(2,1)S(1)}, bf16[12,8,1,8,128]{4,3,2,1,0:T(8,128)(2,1)}, u32[]{:S(2)}) copy-start(bf16[12,8,1,8,128]{4,3,2,1,0:T(8,128)(2,1)} %get-tuple-element.164) | copy-start | bytes 589828
  547.0 12.1 copy-start.1
  559.1 8.8 copy-start.4
  559.1 8.8 copy-start.7
  574.8 731.8 %copy-start.46 = (u32[256]{0:T(256)S(1)}, u32[256]{0:T(256)}, u32[]{:S(2)}) copy-start(u32[256]{0:T(256)} %constant.87) | copy-start | bytes 3076
  574.8 736.5 %copy-start.32 = (pred[12]{0:T(512)(128)(4,1)S(1)}, pred[12]{0:T(512)(128)(4,1)}, u32[]{:S(2)}) copy-start(pred[12]{0:T(512)(128)(4,1)} %copy-done.31) | copy-start | bytes 40
  579.6 19.3 %copy-start.2 = (f32[3456,128]{1,0:T(8,128)S(1)}, f32[3456,128]{1,0:T(8,128)}, u32[]{:S(2)}) copy-start(f32[3456,128]{1,0:T(8,128)} %get-tuple-element.277) | copy-start | bytes 5308420 | tf_op jit(solution)/shard_map/while
  609.1 19.3 %copy-start.2 = (f32[3456,128]{1,0:T(8,128)S(1)}, f32[3456,128]{1,0:T(8,128)}, u32[]{:S(2)}) copy-start(f32[3456,128]{1,0:T(8,128)} %get-tuple-element.277) | copy-start | bytes 5308420 | tf_op jit(solution)/shard_map/while
  638.6 19.3 %copy-start.2 = (f32[3456,128]{1,0:T(8,128)S(1)}, f32[3456,128]{1,0:T(8,128)}, u32[]{:S(2)}) copy-start(f32[3456,128]{1,0:T(8,128)} %get-tuple-element.277) | copy-start | bytes 5308420 | tf_op jit(solution)/shard_map/while
  668.0 19.3 %copy-start.2 = (f32[3456,128]{1,0:T(8,128)S(1)}, f32[3456,128]{1,0:T(8,128)}, u32[]{:S(2)}) copy-start(f32[3456,128]{1,0:T(8,128)} %get-tuple-element.277) | copy-start | bytes 5308420 | tf_op jit(solution)/shard_map/while
  697.5 19.3 %copy-start.2 = (f32[3456,128]{1,0:T(8,128)S(1)}, f32[3456,128]{1,0:T(8,128)}, u32[]{:S(2)}) copy-start(f32[3456,128]{1,0:T(8,128)} %get-tuple-element.277) | copy-start | bytes 5308420 | tf_op jit(solution)/shard_map/while
  727.0 19.3 %copy-start.2 = (f32[3456,128]{1,0:T(8,128)S(1)}, f32[3456,128]{1,0:T(8,128)}, u32[]{:S(2)}) copy-start(f32[3456,128]{1,0:T(8,128)} %get-tuple-element.277) | copy-start | bytes 5308420 | tf_op jit(solution)/shard_map/while
  756.5 19.3 %copy-start.2 = (f32[3456,128]{1,0:T(8,128)S(1)}, f32[3456,128]{1,0:T(8,128)}, u32[]{:S(2)}) copy-start(f32[3456,128]{1,0:T(8,128)} %get-tuple-element.277) | copy-start | bytes 5308420 | tf_op jit(solution)/shard_map/while
  786.0 19.3 %copy-start.2 = (f32[3456,128]{1,0:T(8,128)S(1)}, f32[3456,128]{1,0:T(8,128)}, u32[]{:S(2)}) copy-start(f32[3456,128]{1,0:T(8,128)} %get-tuple-element.277) | copy-start | bytes 5308420 | tf_op jit(solution)/shard_map/while
  815.4 19.3 %copy-start.2 = (f32[3456,128]{1,0:T(8,128)S(1)}, f32[3456,128]{1,0:T(8,128)}, u32[]{:S(2)}) copy-start(f32[3456,128]{1,0:T(8,128)} %get-tuple-element.277) | copy-start | bytes 5308420 | tf_op jit(solution)/shard_map/while
  844.9 19.3 %copy-start.2 = (f32[3456,128]{1,0:T(8,128)S(1)}, f32[3456,128]{1,0:T(8,128)}, u32[]{:S(2)}) copy-start(f32[3456,128]{1,0:T(8,128)} %get-tuple-element.277) | copy-start | bytes 5308420 | tf_op jit(solution)/shard_map/while
  874.4 19.3 %copy-start.2 = (f32[3456,128]{1,0:T(8,128)S(1)}, f32[3456,128]{1,0:T(8,128)}, u32[]{:S(2)}) copy-start(f32[3456,128]{1,0:T(8,128)} %get-tuple-element.277) | copy-start | bytes 5308420 | tf_op jit(solution)/shard_map/while
  903.9 19.3 %copy-start.2 = (f32[3456,128]{1,0:T(8,128)S(1)}, f32[3456,128]{1,0:T(8,128)}, u32[]{:S(2)}) copy-start(f32[3456,128]{1,0:T(8,128)} %get-tuple-element.277) | copy-start | bytes 5308420 | tf_op jit(solution)/shard_map/while
  928.6 382.7 %copy-start.6 = (bf16[12,512,128]{2,1,0:T(8,128)(2,1)S(1)}, bf16[12,512,128]{2,1,0:T(8,128)(2,1)}, u32[]{:S(2)}) copy-start(bf16[12,512,128]{2,1,0:T(8,128)(2,1)} %get-tuple-element.37) | copy-start | bytes 4718596
  1225.5 8.6 collective-permute-start.10
  1226.8 14.3 %collective-permute-start.11 = (f32[32,128]{1,0:T(8,128)S(1)}, f32[32,128]{1,0:T(8,128)S(1)}, u32[]{:S(2)}, u32[]{:S(2)}) collective-permute-start(f32[32,128]{1,0:T(8,128)S(1)} %fusion), channel_id=1, source_target_pairs={{0,16},{2,18},{4,20},{6,22},{8,24},{10,26},{12,28},{14,30},{16,32}... | collective-permute-start | bytes 49160
  1228.1 14.3 %collective-permute-start.12 = (f32[32,128]{1,0:T(8,128)S(1)}, f32[32,128]{1,0:T(8,128)S(1)}, u32[]{:S(2)}, u32[]{:S(2)}) collective-permute-start(f32[32,128]{1,0:T(8,128)S(1)} %fusion), channel_id=1, source_target_pairs={{0,18},{2,20},{4,22},{6,24},{8,26},{10,28},{12,30},{14,32},{16,34}... | collective-permute-start | bytes 49160
  1229.4 14.3 %collective-permute-start.13 = (f32[32,128]{1,0:T(8,128)S(1)}, f32[32,128]{1,0:T(8,128)S(1)}, u32[]{:S(2)}, u32[]{:S(2)}) collective-permute-start(f32[32,128]{1,0:T(8,128)S(1)} %fusion), channel_id=1, source_target_pairs={{0,20},{2,22},{4,24},{6,26},{8,28},{10,30},{12,32},{14,34},{16,36}... | collective-permute-start | bytes 49160
  1230.7 2.1 collective-permute-start.23
  1232.8 16.7 %collective-permute-start.14 = (f32[32,128]{1,0:T(8,128)S(1)}, f32[32,128]{1,0:T(8,128)S(1)}, u32[]{:S(2)}, u32[]{:S(2)}) collective-permute-start(f32[32,128]{1,0:T(8,128)S(1)} %fusion), channel_id=1, source_target_pairs={{0,22},{2,24},{4,26},{6,28},{8,30},{10,32},{12,34},{14,36},{16,38}... | collective-permute-start | bytes 49160
  1234.1 37.8 %collective-permute-start.15 = (f32[32,128]{1,0:T(8,128)S(1)}, f32[32,128]{1,0:T(8,128)S(1)}, u32[]{:S(2)}, u32[]{:S(2)}) collective-permute-start(f32[32,128]{1,0:T(8,128)S(1)} %fusion), channel_id=1, source_target_pairs={{0,24},{2,26},{4,28},{6,30},{8,32},{10,34},{12,36},{14,38},{16,40}... | collective-permute-start | bytes 49160
  1241.1 33.4 %collective-permute-start.16 = (f32[32,128]{1,0:T(8,128)S(1)}, f32[32,128]{1,0:T(8,128)S(1)}, u32[]{:S(2)}, u32[]{:S(2)}) collective-permute-start(f32[32,128]{1,0:T(8,128)S(1)} %fusion), channel_id=1, source_target_pairs={{0,26},{2,28},{4,30},{6,32},{8,34},{10,36},{12,38},{14,40},{16,42}... | collective-permute-start | bytes 49160
  1242.4 40.0 %collective-permute-start.17 = (f32[32,128]{1,0:T(8,128)S(1)}, f32[32,128]{1,0:T(8,128)S(1)}, u32[]{:S(2)}, u32[]{:S(2)}) collective-permute-start(f32[32,128]{1,0:T(8,128)S(1)} %fusion), channel_id=1, source_target_pairs={{0,28},{2,30},{4,32},{6,34},{8,36},{10,38},{12,40},{14,42},{16,44}... | collective-permute-start | bytes 49160
  1243.7 43.6 %collective-permute-start.18 = (f32[32,128]{1,0:T(8,128)S(1)}, f32[32,128]{1,0:T(8,128)S(1)}, u32[]{:S(2)}, u32[]{:S(2)}) collective-permute-start(f32[32,128]{1,0:T(8,128)S(1)} %fusion), channel_id=1, source_target_pairs={{0,30},{2,32},{4,34},{6,36},{8,38},{10,40},{12,42},{14,44},{16,46}... | collective-permute-start | bytes 49160
  1249.5 40.0 %collective-permute-start.19 = (f32[32,128]{1,0:T(8,128)S(1)}, f32[32,128]{1,0:T(8,128)S(1)}, u32[]{:S(2)}, u32[]{:S(2)}) collective-permute-start(f32[32,128]{1,0:T(8,128)S(1)} %fusion), channel_id=1, source_target_pairs={{0,32},{2,34},{4,36},{6,38},{8,40},{10,42},{12,44},{14,46},{16,48}... | collective-permute-start | bytes 49160
  1272.0 19.5 %collective-permute-start.20 = (f32[32,128]{1,0:T(8,128)S(1)}, f32[32,128]{1,0:T(8,128)S(1)}, u32[]{:S(2)}, u32[]{:S(2)}) collective-permute-start(f32[32,128]{1,0:T(8,128)S(1)} %fusion), channel_id=1, source_target_pairs={{0,34},{2,36},{4,38},{6,40},{8,42},{10,44},{12,46},{14,48},{16,50}... | collective-permute-start | bytes 49160
  1274.5 21.5 %collective-permute-start.21 = (f32[32,128]{1,0:T(8,128)S(1)}, f32[32,128]{1,0:T(8,128)S(1)}, u32[]{:S(2)}, u32[]{:S(2)}) collective-permute-start(f32[32,128]{1,0:T(8,128)S(1)} %fusion), channel_id=1, source_target_pairs={{0,36},{2,38},{4,40},{6,42},{8,44},{10,46},{12,48},{14,50},{16,52}... | collective-permute-start | bytes 49160
  1282.4 18.0 %collective-permute-start.22 = (f32[32,128]{1,0:T(8,128)S(1)}, f32[32,128]{1,0:T(8,128)S(1)}, u32[]{:S(2)}, u32[]{:S(2)}) collective-permute-start(f32[32,128]{1,0:T(8,128)S(1)} %fusion), channel_id=1, source_target_pairs={{0,38},{2,40},{4,42},{6,44},{8,46},{10,48},{12,50},{14,52},{16,54}... | collective-permute-start | bytes 49160
  1287.3 17.1 %collective-permute-start.4 = (f32[32,128]{1,0:T(8,128)S(1)}, f32[32,128]{1,0:T(8,128)S(1)}, u32[]{:S(2)}, u32[]{:S(2)}) collective-permute-start(f32[32,128]{1,0:T(8,128)S(1)} %fusion), channel_id=1, source_target_pairs={{0,2},{2,4},{4,6},{6,8},{8,10},{10,12},{12,14},{14,16},{16,18},{18... | collective-permute-start | bytes 49160
  1289.5 18.4 %collective-permute-start.5 = (f32[32,128]{1,0:T(8,128)S(1)}, f32[32,128]{1,0:T(8,128)S(1)}, u32[]{:S(2)}, u32[]{:S(2)}) collective-permute-start(f32[32,128]{1,0:T(8,128)S(1)} %fusion), channel_id=1, source_target_pairs={{0,4},{2,6},{4,8},{6,10},{8,12},{10,14},{12,16},{14,18},{16,20},{1... | collective-permute-start | bytes 49160
  1291.5 16.4 %collective-permute-start.6 = (f32[32,128]{1,0:T(8,128)S(1)}, f32[32,128]{1,0:T(8,128)S(1)}, u32[]{:S(2)}, u32[]{:S(2)}) collective-permute-start(f32[32,128]{1,0:T(8,128)S(1)} %fusion), channel_id=1, source_target_pairs={{0,6},{2,8},{4,10},{6,12},{8,14},{10,16},{12,18},{14,20},{16,22},{... | collective-permute-start | bytes 49160
  1296.1 11.9 collective-permute-start.7
  1300.4 7.5 collective-permute-start.8
  1304.4 3.5 collective-permute-start.9
  (30 other events, 139.6 us)
Sparse Core Ops, SparseCore 0:
  1311.4 71.0 reduce-scatter.5
where the time goes:
time: 1390 us
  blocking collectives  651 us (47%)
  local copies, waits for them, and re-layouts  392 us (28%)
  other arithmetic  94.9 us (7%)
  starting transfers between devices  92.6 us (7%)
  matrix products  71.2 us (5%)
  waiting for transfers between devices  70.8 us (5%)
  between operations  15.7 us (1%)
    unnamed x1, blocking collectives  297 us
    all_gather x1, blocking collectives, on_device(): gathered_rows = lax.all_gather(filt, 'space', axis=0, tiled=True)  295 us
    while x672, local copies, waits for them, and re-layouts  256 us
    gather x54, local copies, waits for them, and re-layouts, assemble(): fetched = jnp.take(source, indices[:, tap], axis=0)  97.3 us
    unnamed x21, starting transfers between devices  80 us
    unnamed x22, waiting for transfers between devices  70.8 us
    all_gather x1, blocking collectives, on_device(): full_filter = lax.all_gather(gathered_rows, 'rep', axis=1, tiled=True)  58.8 us
    dot_general x12, matrix products, per_brick(): lax.dot_general(unrolled_act, center, (((0,), (0,)), ((), ())), preferred...  50.3 us
  transfers between devices with their start and end apart: 25, of which 2 were waited for; matrix products, arithmetic and copies ran while one was open for 10% of the time, Pallas kernels for 0%

commit v1 on v0

--- a/solution.py
+++ b/solution.py
@@ -96,7 +96,9 @@
         0.0,
     ).astype(jnp.bfloat16)
     gathered_rows = lax.all_gather(filt, "space", axis=0, tiled=True)
-    full_filter = lax.all_gather(gathered_rows, "rep", axis=1, tiled=True)
+    full_filter = jnp.concatenate(
+        lax.all_to_all(jnp.stack([gathered_rows] * lax.axis_size("rep")), "rep", 0, 0), axis=1
+    )
     filt_flip = (
         full_filter.reshape(27, channels, channels)
         .transpose(0, 2, 1)

time: 1390 us -> 1420 us (1.022)
  starting transfers between devices: 92.6 us -> 154 us
  blocking collectives: 651 us -> 611 us
    all_to_all x0 -> x1, starting transfers between devices: none -> 62 us  [on_device(): lax.all_to_all(jnp.stack([gathered_rows] * lax.axis_size('rep')), 'rep',...]
    all_gather x1 -> x0, blocking collectives: 58.8 us -> none  [on_device(): full_filter = lax.all_gather(gathered_rows, 'rep', axis=1, tiled=True)]
    all_gather x1, blocking collectives: 295 us -> 314 us  [on_device(): gathered_rows = lax.all_gather(filt, 'space', axis=0, tiled=True)]
  transfers between devices with their start and end apart: 25 -> 26, of which waited for: 2 -> 2; matrix products, arithmetic and copies ran while one was open for 10% -> 10% of each run, Pallas kernels for 0% -> 0%
where the time goes in v1:
time: 1420 us
  blocking collectives  611 us (43%)
  local copies, waits for them, and re-layouts  396 us (28%)
  starting transfers between devices  154 us (11%)
  other arithmetic  98.9 us (7%)
  matrix products  71.2 us (5%)
  waiting for transfers between devices  70.4 us (5%)
  between operations  15.7 us (1%)
    all_gather x1, blocking collectives, on_device(): gathered_rows = lax.all_gather(filt, 'space', axis=0, tiled=True)  314 us
    unnamed x1, blocking collectives  297 us
    while x672, local copies, waits for them, and re-layouts  256 us
    gather x54, local copies, waits for them, and re-layouts, assemble(): fetched = jnp.take(source, indices[:, tap], axis=0)  97.1 us
    unnamed x21, starting transfers between devices  79.9 us
    unnamed x22, waiting for transfers between devices  70.4 us
    all_to_all x1, starting transfers between devices, on_device(): lax.all_to_all(jnp.stack([gathered_rows] * lax.axis_size('rep')), 'rep',...  62 us
    dot_general x12, matrix products, per_brick(): lax.dot_general(unrolled_act, center, (((0,), (0,)), ((), ())), preferred...  50.3 us
  transfers between devices with their start and end apart: 26, of which 2 were waited for; matrix products, arithmetic and copies ran while one was open for 10% of the time, Pallas kernels for 0%

profile of v1, /device:TPU:1, one launch (start us, length us, event | category | flops | bytes accessed | tf_op | source)
XLA Modules:
  0.0 1419.9 jit_solution(5518230740062316495)
XLA Ops:
  9.2 3.3 fusion.11
  13.3 5.1 collective-permute-start.3
  21.1 3.6 collective-permute-start.2
  26.7 314.2 %all-gather = bf16[128,27,64]{2,1,0:T(8,128)(2,1)} all-gather(bf16[1,27,64]{2,1,0:T(8,128)(2,1)S(1)} %bitcast.212), channel_id=1, replica_groups=mesh['space'=128,'rep'=2] {'space'}, dimensions={0}, use_global_device_ids=true | all-gather | bytes 445824 | tf_op jit(solution)/shard_map/all_gather | solution.py:98
  340.9 2.2 stack.7
  343.2 3.1 pad_maximum_fusion
  346.2 2.5 copy.11
  348.8 62.0 %all-to-all-start = ((bf16[2,3456,64]{1,2,0:T(8,128)(2,1)}), bf16[2,3456,64]{1,2,0:T(8,128)(2,1)}, u32[]{:S(2)}, u32[]{:S(2)}) async-start(bf16[2,3456,64]{1,2,0:T(8,128)(2,1)} %copy.11), calls=%async_computation | async-start | bytes 1769472 | tf_op jit(solution)/shard_map/all_to_all | solution.py:100
  423.3 2.0 gather_fusion.12
  425.9 2.0 gather_fusion.41
  451.0 2.0 gather_fusion.11
  479.8 2.0 gather_fusion.40
  499.3 3.5 select_select_fusion
  502.9 4.8 broadcast_select_fusion.4
  507.7 2.3 fusion.12
  510.0 2.2 broadcast_select_fusion.32
  512.3 2.2 broadcast_select_fusion.28
  517.5 2.2 gather_fusion.21
  519.7 2.2 gather_fusion.23
  523.1 2.2 gather_fusion.19
  526.6 2.2 gather_fusion.25
  530.0 2.2 gather_fusion.18
  533.4 2.2 gather_fusion.20
  536.8 2.2 gather_fusion.24
  540.3 2.2 gather_fusion.26
  544.9 2.2 gather_fusion.5
  547.1 2.2 gather_fusion.3
  550.6 2.2 gather_fusion.7
  554.0 2.2 gather_fusion.1
  557.4 2.2 gather_fusion.6
  560.9 2.2 gather_fusion.8
  564.3 2.2 gather_fusion
  567.7 2.2 gather_fusion.22
  571.2 2.2 gather_fusion.4
  574.6 2.2 gather_fusion.2
  588.9 8.8 maximum_maximum_fusion.1
  597.7 6.8 maximum_maximum_fusion
  604.5 353.8 %while.14 = (s32[]{:T(128)}, f32[3456,128]{1,0:T(8,128)}, bf16[12,512,128]{2,1,0:T(8,128)(2,1)}, bf16[12,10,10,10,128]{4,3,2,1,0:T(8,128)(2,1)}, bf16[12,10,10,1...) while((s32[]{:T(128)}, f32[3456,128]{1,0:T(8,128)}, ...), condition=%wide.region_1.4_spmd.clone.clone, body=%wide.region_0.3_spmd.clone.sunk.clone | while | flops 906854400 | bytes 41230984 | solution.py:83
  628.6 4.2 fusion.52
  658.1 4.2 fusion.52
  687.6 4.2 fusion.52
  717.1 4.2 fusion.52
  746.5 4.2 fusion.52
  776.0 4.2 fusion.52
  805.5 4.2 fusion.52
  835.0 4.2 fusion.52
  864.5 4.2 fusion.52
  893.9 4.2 fusion.52
  923.4 4.2 fusion.52
  952.9 4.2 fusion.52
  958.3 296.8 %fusion = f32[32,128]{1,0:T(8,128)S(1)} fusion(f32[3456,128]{1,0:T(8,128)} %get-tuple-element.38), kind=kCustom, calls=%all-reduce-scatter | all-reduce-scatter fusion | flops 524289 | bytes 1786880
  1263.7 6.9 collective-permute-start.15
  1273.2 6.1 collective-permute-start.18
  1279.3 22.1 %collective-permute-start.19 = (f32[32,128]{1,0:T(8,128)S(1)}, f32[32,128]{1,0:T(8,128)S(1)}, u32[]{:S(2)}, u32[]{:S(2)}) collective-permute-start(f32[32,128]{1,0:T(8,128)S(1)} %fusion), channel_id=1, source_target_pairs={{0,32},{2,34},{4,36},{6,38},{8,40},{10,42},{12,44},{14,46},{16,48}... | collective-permute-start | bytes 49160
  1301.4 2.5 collective-permute-start.20
  1304.0 7.8 collective-permute-start.21
  1311.9 4.9 collective-permute-start.22
  1316.8 2.2 collective-permute-start.4
  1321.0 4.6 collective-permute-start.6
  1325.5 4.3 collective-permute-start.7
  1329.9 4.0 collective-permute-start.8
  1333.9 2.2 collective-permute-start.9
  1337.4 2.6 concatenate.112
  1342.1 69.4 %reduce-scatter.6.cloned.1.call-done = f32[64,27]{1,0:T(8,128)} async-done(((f32[128,27]{1,0:T(8,128)}), f32[64,27]{1,0:T(8,128)}) %reduce-scatter.6.cloned.1.call-update) | async-done | bytes 6928
  (982 shorter events, 441.3 us)
Async XLA Ops:
  7.2 11.2 copy-start
  7.2 19.5 %copy-start.15 = (bf16[27,64]{1,0:T(8,128)(2,1)S(1)}, bf16[27,64]{1,0:T(8,128)(2,1)}, u32[]{:S(2)}) copy-start(bf16[27,64]{1,0:T(8,128)(2,1)} %param.15) | copy-start | bytes 10372
  13.3 501.7 %collective-permute-start.3 = (bf16[12,1,8,8,128]{4,3,2,1,0:T(8,128)(2,1)}, bf16[12,1,8,8,128]{4,3,2,1,0:T(8,128)(2,1)S(1)}, u32[]{:S(2)}, u32[]{:S(2)}) collective-permute-start(bf16[12,1,8,8,128]{4,3,2,1,0:T(8,128)(2,1)} %get-tuple-element.129), channel_id=1, source_target_pairs={{1,0},{2,1},{3,2},{4,3},{5,4},{6,5},{7,6},{8,7},{9,8},{10,9},{11,1... | collective-permute-start | bytes 589832 | tf_op jit(solution)/shard_map/ppermute | solution.py:19
  19.2 498.3 %collective-permute-start.1 = (bf16[12,1,8,8,128]{4,3,2,1,0:T(8,128)(2,1)}, bf16[12,1,8,8,128]{4,3,2,1,0:T(8,128)(2,1)}, u32[]{:S(2)}, u32[]{:S(2)}) collective-permute-start(bf16[12,1,8,8,128]{4,3,2,1,0:T(8,128)(2,1)} %get-tuple-element.131), channel_id=1, source_target_pairs={{1,0},{2,1},{3,2},{4,3},{5,4},{6,5},{7,6},{8,7},{9,8},{10,9},{11,1... | collective-permute-start | bytes 589832 | tf_op jit(solution)/shard_map/ppermute | solution.py:19
  21.1 521.3 %collective-permute-start.2 = (bf16[12,1,8,8,128]{4,3,2,1,0:T(8,128)(2,1)}, bf16[12,1,8,8,128]{4,3,2,1,0:T(8,128)(2,1)S(1)}, u32[]{:S(2)}, u32[]{:S(2)}) collective-permute-start(bf16[12,1,8,8,128]{4,3,2,1,0:T(8,128)(2,1)} %get-tuple-element.128), channel_id=1, source_target_pairs={{0,1},{1,2},{2,3},{3,4},{4,5},{5,6},{6,7},{7,8},{8,9},{9,10},{10,1... | collective-permute-start | bytes 589832 | tf_op jit(solution)/shard_map/ppermute | solution.py:19
  24.8 520.2 %collective-permute-start = (bf16[12,1,8,8,128]{4,3,2,1,0:T(8,128)(2,1)}, bf16[12,1,8,8,128]{4,3,2,1,0:T(8,128)(2,1)}, u32[]{:S(2)}, u32[]{:S(2)}) collective-permute-start(bf16[12,1,8,8,128]{4,3,2,1,0:T(8,128)(2,1)} %get-tuple-element.130), channel_id=1, source_target_pairs={{0,1},{1,2},{2,3},{3,4},{4,5},{5,6},{6,7},{7,8},{8,9},{9,10},{10,1... | collective-permute-start | bytes 589832 | tf_op jit(solution)/shard_map/ppermute | solution.py:19
  343.2 67.6 %copy-start.14 = (s32[12,27]{1,0:T(8,128)S(1)}, s32[12,27]{1,0:T(8,128)}, u32[]{:S(2)}) copy-start(s32[12,27]{1,0:T(8,128)} %param.17) | copy-start | bytes 3892
  348.8 148.3 %all-to-all-start = ((bf16[2,3456,64]{1,2,0:T(8,128)(2,1)}), bf16[2,3456,64]{1,2,0:T(8,128)(2,1)}, u32[]{:S(2)}, u32[]{:S(2)}) async-start(bf16[2,3456,64]{1,2,0:T(8,128)(2,1)} %copy.11), calls=%async_computation | async-start | bytes 1769472 | tf_op jit(solution)/shard_map/all_to_all | solution.py:100
  410.8 1000.8 %reduce-scatter.6.cloned.1.call-start = ((), (), s32[]{:S(2)}) async-start(), calls=%async_computation.2 | async-start | bytes 98304
  411.9 9.4 copy-start.38
  472.0 24.4 %copy-start.24 = (s32[12]{0:T(128)S(1)}, s32[12]{0:T(128)}, u32[]{:S(2)}) copy-start(s32[12]{0:T(128)} %get-tuple-element.86) | copy-start | bytes 148
  481.8 17.5 %copy-start.30 = (pred[12]{0:T(512)(128)(4,1)S(1)}, pred[12]{0:T(512)(128)(4,1)}, u32[]{:S(2)}) copy-start(pred[12]{0:T(512)(128)(4,1)} %get-tuple-element.101) | copy-start | bytes 40
  481.8 17.5 %copy-start.31 = (pred[12]{0:T(512)(128)(4,1)S(1)}, pred[12]{0:T(512)(128)(4,1)}, u32[]{:S(2)}) copy-start(pred[12]{0:T(512)(128)(4,1)} %get-tuple-element.202) | copy-start | bytes 40
  502.8 9.4 copy-start.18
  502.9 9.4 copy-start.19
  502.9 9.4 copy-start.36
  502.9 9.4 copy-start.37
  502.9 11.6 copy-start.25
  556.2 26.3 %copy-start.17 = (pred[12]{0:T(512)(128)(4,1)S(1)}, pred[12]{0:T(512)(128)(4,1)}, u32[]{:S(2)}) copy-start(pred[12]{0:T(512)(128)(4,1)} %get-tuple-element.89) | copy-start | bytes 40
  556.2 27.3 %copy-start.16 = (pred[12]{0:T(512)(128)(4,1)S(1)}, pred[12]{0:T(512)(128)(4,1)}, u32[]{:S(2)}) copy-start(pred[12]{0:T(512)(128)(4,1)} %get-tuple-element.94) | copy-start | bytes 40
  567.7 21.1 %copy-start.5 = (bf16[12,8,8,1,128]{4,3,2,1,0:T(2,128)(2,1)S(1)}, bf16[12,8,8,1,128]{4,3,2,1,0:T(2,128)(2,1)}, u32[]{:S(2)}) copy-start(bf16[12,8,8,1,128]{4,3,2,1,0:T(2,128)(2,1)} %get-tuple-element.160) | copy-start | bytes 589828
  574.6 14.2 copy-start.9
  576.8 12.0 copy-start.1
  588.8 8.8 copy-start.4
  588.8 8.8 copy-start.7
  588.8 8.8 copy-start.8
  588.8 8.8 copy-start.10
  588.8 8.8 copy-start.11
  588.8 8.8 copy-start.12
  604.5 731.6 %copy-start.41 = (u32[256]{0:T(256)S(1)}, u32[256]{0:T(256)}, u32[]{:S(2)}) copy-start(u32[256]{0:T(256)} %constant.87) | copy-start | bytes 3076
  604.5 736.3 %copy-start.27 = (pred[12]{0:T(512)(128)(4,1)S(1)}, pred[12]{0:T(512)(128)(4,1)}, u32[]{:S(2)}) copy-start(pred[12]{0:T(512)(128)(4,1)} %copy-done.26) | copy-start | bytes 40
  609.3 19.3 %copy-start.2 = (f32[3456,128]{1,0:T(8,128)S(1)}, f32[3456,128]{1,0:T(8,128)}, u32[]{:S(2)}) copy-start(f32[3456,128]{1,0:T(8,128)} %get-tuple-element.277) | copy-start | bytes 5308420 | tf_op jit(solution)/shard_map/while
  638.8 19.3 %copy-start.2 = (f32[3456,128]{1,0:T(8,128)S(1)}, f32[3456,128]{1,0:T(8,128)}, u32[]{:S(2)}) copy-start(f32[3456,128]{1,0:T(8,128)} %get-tuple-element.277) | copy-start | bytes 5308420 | tf_op jit(solution)/shard_map/while
  668.3 19.3 %copy-start.2 = (f32[3456,128]{1,0:T(8,128)S(1)}, f32[3456,128]{1,0:T(8,128)}, u32[]{:S(2)}) copy-start(f32[3456,128]{1,0:T(8,128)} %get-tuple-element.277) | copy-start | bytes 5308420 | tf_op jit(solution)/shard_map/while
  697.7 19.3 %copy-start.2 = (f32[3456,128]{1,0:T(8,128)S(1)}, f32[3456,128]{1,0:T(8,128)}, u32[]{:S(2)}) copy-start(f32[3456,128]{1,0:T(8,128)} %get-tuple-element.277) | copy-start | bytes 5308420 | tf_op jit(solution)/shard_map/while
  727.2 19.3 %copy-start.2 = (f32[3456,128]{1,0:T(8,128)S(1)}, f32[3456,128]{1,0:T(8,128)}, u32[]{:S(2)}) copy-start(f32[3456,128]{1,0:T(8,128)} %get-tuple-element.277) | copy-start | bytes 5308420 | tf_op jit(solution)/shard_map/while
  756.7 19.3 %copy-start.2 = (f32[3456,128]{1,0:T(8,128)S(1)}, f32[3456,128]{1,0:T(8,128)}, u32[]{:S(2)}) copy-start(f32[3456,128]{1,0:T(8,128)} %get-tuple-element.277) | copy-start | bytes 5308420 | tf_op jit(solution)/shard_map/while
  786.2 19.3 %copy-start.2 = (f32[3456,128]{1,0:T(8,128)S(1)}, f32[3456,128]{1,0:T(8,128)}, u32[]{:S(2)}) copy-start(f32[3456,128]{1,0:T(8,128)} %get-tuple-element.277) | copy-start | bytes 5308420 | tf_op jit(solution)/shard_map/while
  815.7 19.3 %copy-start.2 = (f32[3456,128]{1,0:T(8,128)S(1)}, f32[3456,128]{1,0:T(8,128)}, u32[]{:S(2)}) copy-start(f32[3456,128]{1,0:T(8,128)} %get-tuple-element.277) | copy-start | bytes 5308420 | tf_op jit(solution)/shard_map/while
  845.1 19.3 %copy-start.2 = (f32[3456,128]{1,0:T(8,128)S(1)}, f32[3456,128]{1,0:T(8,128)}, u32[]{:S(2)}) copy-start(f32[3456,128]{1,0:T(8,128)} %get-tuple-element.277) | copy-start | bytes 5308420 | tf_op jit(solution)/shard_map/while
  874.6 19.3 %copy-start.2 = (f32[3456,128]{1,0:T(8,128)S(1)}, f32[3456,128]{1,0:T(8,128)}, u32[]{:S(2)}) copy-start(f32[3456,128]{1,0:T(8,128)} %get-tuple-element.277) | copy-start | bytes 5308420 | tf_op jit(solution)/shard_map/while
  904.1 19.3 %copy-start.2 = (f32[3456,128]{1,0:T(8,128)S(1)}, f32[3456,128]{1,0:T(8,128)}, u32[]{:S(2)}) copy-start(f32[3456,128]{1,0:T(8,128)} %get-tuple-element.277) | copy-start | bytes 5308420 | tf_op jit(solution)/shard_map/while
  933.6 19.3 %copy-start.2 = (f32[3456,128]{1,0:T(8,128)S(1)}, f32[3456,128]{1,0:T(8,128)}, u32[]{:S(2)}) copy-start(f32[3456,128]{1,0:T(8,128)} %get-tuple-element.277) | copy-start | bytes 5308420 | tf_op jit(solution)/shard_map/while
  958.3 382.5 %copy-start.6 = (bf16[12,512,128]{2,1,0:T(8,128)(2,1)S(1)}, bf16[12,512,128]{2,1,0:T(8,128)(2,1)}, u32[]{:S(2)}) copy-start(bf16[12,512,128]{2,1,0:T(8,128)(2,1)} %get-tuple-element.37) | copy-start | bytes 4718596
  1255.1 8.6 collective-permute-start.10
  1256.4 14.2 %collective-permute-start.11 = (f32[32,128]{1,0:T(8,128)S(1)}, f32[32,128]{1,0:T(8,128)S(1)}, u32[]{:S(2)}, u32[]{:S(2)}) collective-permute-start(f32[32,128]{1,0:T(8,128)S(1)} %fusion), channel_id=1, source_target_pairs={{0,16},{2,18},{4,20},{6,22},{8,24},{10,26},{12,28},{14,30},{16,32}... | collective-permute-start | bytes 49160
  1257.7 14.2 %collective-permute-start.12 = (f32[32,128]{1,0:T(8,128)S(1)}, f32[32,128]{1,0:T(8,128)S(1)}, u32[]{:S(2)}, u32[]{:S(2)}) collective-permute-start(f32[32,128]{1,0:T(8,128)S(1)} %fusion), channel_id=1, source_target_pairs={{0,18},{2,20},{4,22},{6,24},{8,26},{10,28},{12,30},{14,32},{16,34}... | collective-permute-start | bytes 49160
  1259.0 14.2 %collective-permute-start.13 = (f32[32,128]{1,0:T(8,128)S(1)}, f32[32,128]{1,0:T(8,128)S(1)}, u32[]{:S(2)}, u32[]{:S(2)}) collective-permute-start(f32[32,128]{1,0:T(8,128)S(1)} %fusion), channel_id=1, source_target_pairs={{0,20},{2,22},{4,24},{6,26},{8,28},{10,30},{12,32},{14,34},{16,36}... | collective-permute-start | bytes 49160
  1260.3 2.1 collective-permute-start.23
  1262.4 16.9 %collective-permute-start.14 = (f32[32,128]{1,0:T(8,128)S(1)}, f32[32,128]{1,0:T(8,128)S(1)}, u32[]{:S(2)}, u32[]{:S(2)}) collective-permute-start(f32[32,128]{1,0:T(8,128)S(1)} %fusion), channel_id=1, source_target_pairs={{0,22},{2,24},{4,26},{6,28},{8,30},{10,32},{12,34},{14,36},{16,38}... | collective-permute-start | bytes 49160
  1263.7 37.7 %collective-permute-start.15 = (f32[32,128]{1,0:T(8,128)S(1)}, f32[32,128]{1,0:T(8,128)S(1)}, u32[]{:S(2)}, u32[]{:S(2)}) collective-permute-start(f32[32,128]{1,0:T(8,128)S(1)} %fusion), channel_id=1, source_target_pairs={{0,24},{2,26},{4,28},{6,30},{8,32},{10,34},{12,36},{14,38},{16,40}... | collective-permute-start | bytes 49160
  1270.6 33.4 %collective-permute-start.16 = (f32[32,128]{1,0:T(8,128)S(1)}, f32[32,128]{1,0:T(8,128)S(1)}, u32[]{:S(2)}, u32[]{:S(2)}) collective-permute-start(f32[32,128]{1,0:T(8,128)S(1)} %fusion), channel_id=1, source_target_pairs={{0,26},{2,28},{4,30},{6,32},{8,34},{10,36},{12,38},{14,40},{16,42}... | collective-permute-start | bytes 49160
  1271.9 40.0 %collective-permute-start.17 = (f32[32,128]{1,0:T(8,128)S(1)}, f32[32,128]{1,0:T(8,128)S(1)}, u32[]{:S(2)}, u32[]{:S(2)}) collective-permute-start(f32[32,128]{1,0:T(8,128)S(1)} %fusion), channel_id=1, source_target_pairs={{0,28},{2,30},{4,32},{6,34},{8,36},{10,38},{12,40},{14,42},{16,44}... | collective-permute-start | bytes 49160
  1273.2 43.6 %collective-permute-start.18 = (f32[32,128]{1,0:T(8,128)S(1)}, f32[32,128]{1,0:T(8,128)S(1)}, u32[]{:S(2)}, u32[]{:S(2)}) collective-permute-start(f32[32,128]{1,0:T(8,128)S(1)} %fusion), channel_id=1, source_target_pairs={{0,30},{2,32},{4,34},{6,36},{8,38},{10,40},{12,42},{14,44},{16,46}... | collective-permute-start | bytes 49160
  1279.3 39.7 %collective-permute-start.19 = (f32[32,128]{1,0:T(8,128)S(1)}, f32[32,128]{1,0:T(8,128)S(1)}, u32[]{:S(2)}, u32[]{:S(2)}) collective-permute-start(f32[32,128]{1,0:T(8,128)S(1)} %fusion), channel_id=1, source_target_pairs={{0,32},{2,34},{4,36},{6,38},{8,40},{10,42},{12,44},{14,46},{16,48}... | collective-permute-start | bytes 49160
  1301.4 19.5 %collective-permute-start.20 = (f32[32,128]{1,0:T(8,128)S(1)}, f32[32,128]{1,0:T(8,128)S(1)}, u32[]{:S(2)}, u32[]{:S(2)}) collective-permute-start(f32[32,128]{1,0:T(8,128)S(1)} %fusion), channel_id=1, source_target_pairs={{0,34},{2,36},{4,38},{6,40},{8,42},{10,44},{12,46},{14,48},{16,50}... | collective-permute-start | bytes 49160
  1304.0 21.5 %collective-permute-start.21 = (f32[32,128]{1,0:T(8,128)S(1)}, f32[32,128]{1,0:T(8,128)S(1)}, u32[]{:S(2)}, u32[]{:S(2)}) collective-permute-start(f32[32,128]{1,0:T(8,128)S(1)} %fusion), channel_id=1, source_target_pairs={{0,36},{2,38},{4,40},{6,42},{8,44},{10,46},{12,48},{14,50},{16,52}... | collective-permute-start | bytes 49160
  1311.9 18.0 %collective-permute-start.22 = (f32[32,128]{1,0:T(8,128)S(1)}, f32[32,128]{1,0:T(8,128)S(1)}, u32[]{:S(2)}, u32[]{:S(2)}) collective-permute-start(f32[32,128]{1,0:T(8,128)S(1)} %fusion), channel_id=1, source_target_pairs={{0,38},{2,40},{4,42},{6,44},{8,46},{10,48},{12,50},{14,52},{16,54}... | collective-permute-start | bytes 49160
  1316.8 17.1 %collective-permute-start.4 = (f32[32,128]{1,0:T(8,128)S(1)}, f32[32,128]{1,0:T(8,128)S(1)}, u32[]{:S(2)}, u32[]{:S(2)}) collective-permute-start(f32[32,128]{1,0:T(8,128)S(1)} %fusion), channel_id=1, source_target_pairs={{0,2},{2,4},{4,6},{6,8},{8,10},{10,12},{12,14},{14,16},{16,18},{18... | collective-permute-start | bytes 49160
  1319.0 18.4 %collective-permute-start.5 = (f32[32,128]{1,0:T(8,128)S(1)}, f32[32,128]{1,0:T(8,128)S(1)}, u32[]{:S(2)}, u32[]{:S(2)}) collective-permute-start(f32[32,128]{1,0:T(8,128)S(1)} %fusion), channel_id=1, source_target_pairs={{0,4},{2,6},{4,8},{6,10},{8,12},{10,14},{12,16},{14,18},{16,20},{1... | collective-permute-start | bytes 49160
  1321.0 16.4 %collective-permute-start.6 = (f32[32,128]{1,0:T(8,128)S(1)}, f32[32,128]{1,0:T(8,128)S(1)}, u32[]{:S(2)}, u32[]{:S(2)}) collective-permute-start(f32[32,128]{1,0:T(8,128)S(1)} %fusion), channel_id=1, source_target_pairs={{0,6},{2,8},{4,10},{6,12},{8,14},{10,16},{12,18},{14,20},{16,22},{... | collective-permute-start | bytes 49160
  1325.5 11.9 collective-permute-start.7
  1329.9 7.5 collective-permute-start.8
  1333.9 3.5 collective-permute-start.9
  (26 other events, 104.4 us)
Sparse Core Ops, SparseCore 0:
  1340.9 70.6 reduce-scatter.5
